TPU v7x, 256 devices: a whole 4x4x8 slice. The times are simulated.
256 devices in a mesh: row: 16 (over x, y), col: 16 (over z, core).
Axes of the slice: x: 4, y: 4, z: 8, core: 2. Of those that a mesh axis runs over, the one named last changes fastest.
Arguments:
- coefficients: float32 [4096, 4096], P('row', 'col'), may hold values from -6 to 6
- diagonal: float32 [4096, 4096], P('row', 'col'), may hold values from 1.5 to 6
- energy_shift: float32 [1], replicated, may hold values from -1 to 0
- integrals: float32 [484, 484], replicated, may hold values from -0.25 to 0.25
- source_row: int32 [256, 128], P('row'), may hold values from 0 to 255
- target_row: int32 [256, 128], P('row'), may hold values from 0 to 7743
- phase_row: int32 [256, 128], P('row'), may hold values from -1 to 1, as said below
- source_col: int32 [256, 128], P('col'), may hold values from 0 to 255
- target_col: int32 [256, 128], P('col'), may hold values from 0 to 7743
- phase_col: int32 [256, 128], P('col'), may hold values from -1 to 1, as said below
Outputs:
- sigma_vector: float32 [4096, 4096], P('row', 'col')
- correction: float32 [4096, 4096], P('row', 'col')
Inputs may be any that keep to these rules, and one draw needn't show every extreme that they name: `phase_row`: in each list row the entries with sign -1 or 1 come first and the rest are 0; in every draw some owner block receives all 128 slots live from every alpha block. `phase_col`: in each list row the entries with sign -1 or 1 come first and the rest are 0; in every draw some owner block receives all 128 slots live from every beta block.
All inputs are finite; a program needn't handle non-finite values.
Results may differ from a plain program's by a relative error of at most 0.000055.
Values sent between devices are 32-bit elements; how exact they have to be, the bound alone decides.
A program may use at most 64 MiB of HBM per device.

v0:
```python
import jax
import jax.numpy as jnp
from jax import lax
from jax.sharding import PartitionSpec as P

K_DEV = 16


def entry_table(source, target, phases, my_index, rows_dev):
    global_row = my_index * rows_dev + source
    return jnp.stack([target, global_row, phases], axis=1)


def signed_rows(block, source, phases):
    return block[source] * phases[..., None].astype(jnp.float32)


def owner_products(received, entry_meta, integrals):
    lane_count = received.shape[-1]
    pair_count = integrals.shape[0]
    places = entry_meta[:, 0, :].reshape(-1)
    densities = (
        jnp.zeros((K_DEV * pair_count, lane_count), jnp.float32)
        .at[places]
        .add(received.reshape(-1, lane_count))
    )
    products = jnp.einsum(
        "ip,kpb->kib",
        integrals,
        densities.reshape(-1, pair_count, lane_count),
        precision=lax.Precision.HIGHEST,
    ).reshape(-1, lane_count)
    return products[entry_meta[:, 0, :]] * entry_meta[:, 2, :, None].astype(jnp.float32)


def local_terms(picked, entry_meta, first_row, row_count):
    lane_count = picked.shape[-1]
    offset = entry_meta[:, 1, :].reshape(-1) - first_row
    inside = ((offset >= 0) & (offset < row_count)).astype(jnp.float32)
    flat_rows = picked.reshape(-1, lane_count) * inside[:, None]
    return (
        jnp.zeros((row_count, lane_count), jnp.float32)
        .at[jnp.clip(offset, 0, row_count - 1)]
        .add(flat_rows)
    )


def alpha_sigma(block, source, target, phases, integrals):
    row_count = block.shape[0]
    entry_meta = entry_table(source, target, phases, lax.axis_index("row"), row_count)
    received, meta_in = (
        lax.all_to_all(
            signed_rows(block, source, phases), "row", split_axis=0, concat_axis=0, tiled=True
        ),
        lax.all_to_all(entry_meta, "row", split_axis=0, concat_axis=0, tiled=True),
    )
    picked = owner_products(received, meta_in, integrals)
    return lax.psum_scatter(
        local_terms(picked, meta_in, jnp.int32(0), lax.axis_size("row") * row_count),
        "row",
        scatter_dimension=0,
        tiled=True,
    )


def beta_sigma(block, source, target, phases, integrals):
    row_count = block.shape[0]
    entry_meta = entry_table(source, target, phases, lax.axis_index("col"), row_count)
    received, meta_in = (
        lax.all_to_all(
            signed_rows(block, source, phases), "col", split_axis=0, concat_axis=0, tiled=True
        ),
        lax.all_to_all(entry_meta, "col", split_axis=0, concat_axis=0, tiled=True),
    )
    picked = owner_products(received, meta_in, integrals)
    return lax.psum_scatter(
        local_terms(picked, meta_in, jnp.int32(0), lax.axis_size("col") * row_count),
        "col",
        scatter_dimension=0,
        tiled=True,
    )


def shards(
    coefficients,
    diagonal,
    energy_shift,
    integrals,
    source_row,
    target_row,
    phase_row,
    source_col,
    target_col,
    phase_col,
):
    alpha_part = alpha_sigma(coefficients, source_row, target_row, phase_row, integrals)
    beta_part = beta_sigma(coefficients.T, source_col, target_col, phase_col, integrals)
    sigma_vector = alpha_part + beta_part.T
    correction = (sigma_vector - energy_shift[0] * coefficients) / (diagonal - energy_shift[0])
    return (sigma_vector, correction)


def solution(mesh):
    in_specs = (
        P("row", "col"),
        P("row", "col"),
        P(),
        P(),
        P("row", None),
        P("row", None),
        P("row", None),
        P("col", None),
        P("col", None),
        P("col", None),
    )
    out_specs = (P("row", "col"), P("row", "col"))
    return jax.shard_map(shards, mesh=mesh, in_specs=in_specs, out_specs=out_specs, check_vma=False)
```

profile of v0, /device:TPU:1, one launch (start us, length us, event | category | flops | bytes accessed | tf_op | source)
XLA Modules:
  0.0 359.0 jit_solution(16216809859217844449)
XLA Ops:
  7.2 0.8 broadcast_add_fusion.1
  8.0 1.4 pad_add_fusion
  9.3 7.6 %all-to-all-start = ((s32[16,3,128]{2,1,0:T(4,128)}), s32[16,3,128]{2,1,0:T(4,128)S(1)}, u32[]{:S(2)}, u32[]{:S(2)}) async-start(s32[16,3,128]{2,1,0:T(4,128)} %pad_add_fusion), calls=%async_computation | async-start | bytes 65536 | tf_op jit(solution)/shard_map/all_to_all | solution.py:55
  16.9 0.7 fusion.19
  17.6 0.7 convert_element_type.50
  18.3 7.6 %gather_fusion = f32[2048,256]{1,0:T(8,128)S(1)} fusion(f32[256,256]{1,0:T(8,128)} %param.10, s32[2048]{0:T(1024)S(1)} %fusion.19), kind=kCustom, calls=%fused_computation | custom fusion | bytes 4202496 | tf_op jit(solution)/shard_map/gather | solution.py:15
  25.9 1.7 broadcast_multiply_fusion.1
  27.6 6.7 %all-to-all-start.1 = ((f32[16,128,256]{2,1,0:T(8,128)}), f32[16,128,256]{2,1,0:T(8,128)S(1)}, u32[]{:S(2)}, u32[]{:S(2)}) async-start(f32[16,128,256]{2,1,0:T(8,128)} %broadcast_multiply_fusion.1), calls=%async_computation.1 | async-start | bytes 4194304 | tf_op jit(solution)/shard_map/all_to_all | solution.py:52
  34.3 0.0 reduce-scatter.3.cloned.1.call-start
  34.4 25.6 %all-to-all-done.1 = f32[16,128,256]{2,1,0:T(8,128)S(1)} async-done(((f32[16,128,256]{2,1,0:T(8,128)}), f32[16,128,256]{2,1,0:T(8,128)S(1)}, u32[]{:S(2)}, u32[]{:S(2)}) %all-to-all-start.1) | async-done | bytes 2097184 | tf_op jit(solution)/shard_map/all_to_all | solution.py:52
  60.0 15.2 %scatter_custom_fusion = f32[7744,256]{1,0:T(8,128)} fusion(s32[2048]{0:T(1024)S(1)} %bitcast.83, f32[2048,256]{1,0:T(8,128)S(1)} %bitcast.67, f32[]{:T(128)} %constant.8.clone.1), kind=kCustom, calls=%fused_computation.10 | custom fusion | flops 524288 | bytes 7929860 | tf_op jit(solution)/shard_map/scatter-add | solution.py:25
  75.2 6.9 %reshape.243 = f32[16,484,256]{2,1,0:T(8,128)} reshape(f32[7744,256]{1,0:T(8,128)} %scatter_custom_fusion) | data formatting | bytes 15859712 | tf_op jit(solution)/shard_map/reshape | solution.py:30
  82.1 16.3 %convolution_bitcast_fusion.1 = f32[16,484,256]{2,1,0:T(8,128)} fusion(f32[16,484,256]{2,1,0:T(8,128)} %reshape.243, f32[484,484]{1,0:T(8,128)S(1)} %copy-done), kind=kOutput, calls=%fused_computation.13 | convolution fusion | flops 11514150912 | bytes 16796736 | tf_op jit(solution)/shard_map/ip,kpb->kib/dot_general | solution.py:27
  98.5 6.9 %reshape.244 = f32[7744,256]{1,0:T(8,128)} reshape(f32[16,484,256]{2,1,0:T(8,128)} %convolution_bitcast_fusion.1) | data formatting | bytes 15859712 | tf_op jit(solution)/shard_map/reshape | solution.py:32
  105.4 27.2 %scatter_custom_fusion.1 = f32[4096,256]{1,0:T(8,128)} fusion(s32[2048]{0:T(1024)S(1)} %bitcast.82, f32[]{:T(128)} %constant.8.clone.1, f32[2048]{0:T(1024)S(1)} %bitcast.76, f32[2048]{0:T(1024)S(1)} %bitcast.78, f32[7744,256]{1,0:T(8,128)} %reshape.244, s32[2048]{0:T(1024)S(1)} %fusion.21), kind=kCustom, calls=%fused_computation.17 | custom fusion | flops 1572864 | bytes 12148740 | tf_op jit(solution)/shard_map/scatter-add | solution.py:44
  132.7 0.7 copy-done.4
  133.4 0.6 pad_add_fusion.1
  134.0 13.6 %all-to-all-start.2 = ((s32[16,3,128]{2,1,0:T(4,128)}), s32[16,3,128]{2,1,0:T(4,128)S(1)}, u32[]{:S(2)}, u32[]{:S(2)}) async-start(s32[16,3,128]{2,1,0:T(4,128)} %pad_add_fusion.1), calls=%async_computation.3 | async-start | bytes 65536 | tf_op jit(solution)/shard_map/all_to_all | solution.py:73
  147.5 0.1 copy.17
  147.7 8.6 %gather_fusion.1 = f32[2048,256]{1,0:T(8,128)} fusion(f32[256,256]{1,0:T(8,128)S(1)} %bitcast.64, s32[2048]{0:T(1024)S(1)} %fusion.23), kind=kCustom, calls=%fused_computation.2 | custom fusion | bytes 4202496 | tf_op jit(solution)/shard_map/gather | solution.py:15
  156.3 3.3 broadcast_multiply_fusion
  159.6 7.2 %all-to-all-start.3 = ((f32[16,128,256]{2,1,0:T(8,128)}), f32[16,128,256]{2,1,0:T(8,128)S(1)}, u32[]{:S(2)}, u32[]{:S(2)}) async-start(f32[16,128,256]{2,1,0:T(8,128)} %broadcast_multiply_fusion), calls=%async_computation.4 | async-start | bytes 4194304 | tf_op jit(solution)/shard_map/all_to_all | solution.py:70
  166.8 0.3 reduce-scatter.5.cloned.1.call-start
  167.1 48.7 %all-to-all-done.3 = f32[16,128,256]{2,1,0:T(8,128)S(1)} async-done(((f32[16,128,256]{2,1,0:T(8,128)}), f32[16,128,256]{2,1,0:T(8,128)S(1)}, u32[]{:S(2)}, u32[]{:S(2)}) %all-to-all-start.3) | async-done | bytes 2097184 | tf_op jit(solution)/shard_map/all_to_all | solution.py:70
  215.8 15.2 %scatter_custom_fusion.2 = f32[7744,256]{1,0:T(8,128)} fusion(s32[2048]{0:T(1024)S(1)} %bitcast.84, f32[2048,256]{1,0:T(8,128)S(1)} %bitcast.68, f32[]{:T(128)} %constant.8.clone.1), kind=kCustom, calls=%fused_computation.8 | custom fusion | flops 524288 | bytes 7929860 | tf_op jit(solution)/shard_map/scatter-add | solution.py:25
  231.0 6.9 %reshape.246 = f32[16,484,256]{2,1,0:T(8,128)} reshape(f32[7744,256]{1,0:T(8,128)} %scatter_custom_fusion.2) | data formatting | bytes 15859712 | tf_op jit(solution)/shard_map/reshape | solution.py:30
  237.9 16.3 %convolution_bitcast_fusion = f32[16,484,256]{2,1,0:T(8,128)} fusion(f32[16,484,256]{2,1,0:T(8,128)} %reshape.246, f32[484,484]{1,0:T(8,128)S(1)} %copy-done), kind=kOutput, calls=%fused_computation.12 | convolution fusion | flops 11514150912 | bytes 16796736 | tf_op jit(solution)/shard_map/ip,kpb->kib/dot_general | solution.py:27
  254.3 6.9 %reshape.247 = f32[7744,256]{1,0:T(8,128)} reshape(f32[16,484,256]{2,1,0:T(8,128)} %convolution_bitcast_fusion) | data formatting | bytes 15859712 | tf_op jit(solution)/shard_map/reshape | solution.py:32
  261.2 27.3 %scatter_custom_fusion.3 = f32[4096,256]{1,0:T(8,128)} fusion(s32[2048]{0:T(1024)S(1)} %bitcast.81, f32[]{:T(128)} %constant.8.clone.1, f32[2048]{0:T(1024)S(1)} %bitcast.75, f32[2048]{0:T(1024)S(1)} %bitcast.77, f32[7744,256]{1,0:T(8,128)} %reshape.247, s32[2048]{0:T(1024)S(1)} %fusion.25), kind=kCustom, calls=%fused_computation.14 | custom fusion | flops 1572864 | bytes 12148740 | tf_op jit(solution)/shard_map/scatter-add | solution.py:44
  288.5 5.6 %copy.18 = f32[4096,256]{0,1:T(8,128)} copy(f32[4096,256]{1,0:T(8,128)} %scatter_custom_fusion.3) | data formatting | bytes 8388608 | tf_op jit(solution)/shard_map/scatter-add | solution.py:44
  294.8 55.4 %reduce-scatter.5.cloned.1.call-done = f32[256,256]{0,1:T(8,128)} async-done(((f32[4096,256]{0,1:T(8,128)}), f32[256,256]{0,1:T(8,128)}) %reduce-scatter.5.cloned.1.call-update) | async-done | bytes 262160 | tf_op jit(solution)/shard_map/reduce_scatter | solution.py:76
  350.3 1.9 subtract_divide_fusion
  (27 shorter events, 0.3 us)
Async XLA Ops:
  7.2 75.0 %copy-start = (f32[484,484]{1,0:T(8,128)S(1)}, f32[484,484]{1,0:T(8,128)}, u32[]{:S(2)}) copy-start(f32[484,484]{1,0:T(8,128)} %param.13) | copy-start | bytes 2811076
  9.3 18.3 %all-to-all-start = ((s32[16,3,128]{2,1,0:T(4,128)}), s32[16,3,128]{2,1,0:T(4,128)S(1)}, u32[]{:S(2)}, u32[]{:S(2)}) async-start(s32[16,3,128]{2,1,0:T(4,128)} %pad_add_fusion), calls=%async_computation | async-start | bytes 65536 | tf_op jit(solution)/shard_map/all_to_all | solution.py:55
  27.6 32.4 %all-to-all-start.1 = ((f32[16,128,256]{2,1,0:T(8,128)}), f32[16,128,256]{2,1,0:T(8,128)S(1)}, u32[]{:S(2)}, u32[]{:S(2)}) async-start(f32[16,128,256]{2,1,0:T(8,128)} %broadcast_multiply_fusion.1), calls=%async_computation.1 | async-start | bytes 4194304 | tf_op jit(solution)/shard_map/all_to_all | solution.py:52
  34.3 260.6 %reduce-scatter.3.cloned.1.call-start = ((), (), s32[]{:S(2)}) async-start(), calls=%async_computation.6 | async-start | bytes 4456448 | tf_op jit(solution)/shard_map/reduce_scatter | solution.py:58
  132.6 0.7 copy-start.4
  132.6 0.7 copy-start.3
  132.6 0.7 copy-start.5
  132.6 14.9 %copy-start.1 = (f32[256,256]{1,0:T(8,128)S(1)}, f32[256,256]{1,0:T(8,128)}, u32[]{:S(2)}) copy-start(f32[256,256]{1,0:T(8,128)} %param.10) | copy-start | bytes 786436
  134.0 25.6 %all-to-all-start.2 = ((s32[16,3,128]{2,1,0:T(4,128)}), s32[16,3,128]{2,1,0:T(4,128)S(1)}, u32[]{:S(2)}, u32[]{:S(2)}) async-start(s32[16,3,128]{2,1,0:T(4,128)} %pad_add_fusion.1), calls=%async_computation.3 | async-start | bytes 65536 | tf_op jit(solution)/shard_map/all_to_all | solution.py:73
  159.6 56.3 %all-to-all-start.3 = ((f32[16,128,256]{2,1,0:T(8,128)}), f32[16,128,256]{2,1,0:T(8,128)S(1)}, u32[]{:S(2)}, u32[]{:S(2)}) async-start(f32[16,128,256]{2,1,0:T(8,128)} %broadcast_multiply_fusion), calls=%async_computation.4 | async-start | bytes 4194304 | tf_op jit(solution)/shard_map/all_to_all | solution.py:70
  166.8 183.5 %reduce-scatter.5.cloned.1.call-start = ((), (), s32[]{:S(2)}) async-start(), calls=%async_computation.7 | async-start | bytes 4456448 | tf_op jit(solution)/shard_map/reduce_scatter | solution.py:76
  294.1 56.2 %copy-start.2 = (f32[256,256]{1,0:T(8,128)S(1)}, f32[256,256]{1,0:T(8,128)}, u32[]{:S(2)}) copy-start(f32[256,256]{1,0:T(8,128)} %param.11) | copy-start | bytes 786436
Sparse Core Ops, SparseCore 0:
  132.8 85.9 reduce-scatter.2
  294.2 55.9 reduce-scatter.4
where the time goes:
time: 362 us; the launch traced here: 359 us
  waiting for transfers between devices  130 us (36%)
  other arithmetic  96 us (27%)
  local copies, waits for them, and re-layouts  50.3 us (14%)
  starting transfers between devices  35.3 us (10%)
  matrix products  32.7 us (9%)
  between operations  14.9 us (4%)
    reduce_scatter x1, waiting for transfers between devices, beta_sigma(): lax.psum_scatter(local_terms(picked, meta_in, jnp.int32(0), lax.axis_size...  55.4 us
    scatter-add x2, other arithmetic, local_terms(): return jnp.zeros((row_count, lane_count), jnp.float32).at[jnp.clip(offset...  54.5 us
    all_to_all x1, waiting for transfers between devices, beta_sigma(): lax.all_to_all(signed_rows(block, source, phases), 'col', split_axis=0, c...  48.7 us
    dot_general x2, matrix products, owner_products(): jnp.einsum('ip,kpb->kib', integrals, densities.reshape(-1, pair_count, la...  32.7 us
    scatter-add x2, other arithmetic, owner_products(): densities = jnp.zeros((K_DEV * pair_count, lane_count), jnp.float32).at[p...  30.4 us
    all_to_all x1, waiting for transfers between devices, alpha_sigma(): lax.all_to_all(signed_rows(block, source, phases), 'row', split_axis=0, c...  25.6 us
    gather x2, local copies, waits for them, and re-layouts, signed_rows(): return block[source] * phases[..., None].astype(jnp.float32)  16.2 us
    reshape x2, local copies, waits for them, and re-layouts, owner_products(): products = jnp.einsum('ip,kpb->kib', integrals, densities.reshape(-1, pai...  13.9 us
  transfers between devices with their start and end apart: 6, of which 3 were waited for; matrix products, arithmetic and copies ran while one was open for 28% of the time, Pallas kernels for 0%

commit v1 on v0

v1 whole, which is shorter than its diff:
```python
import functools

import jax
import jax.numpy as jnp
from jax import lax
from jax.experimental import pallas as pl
from jax.experimental.pallas import tpu as pltpu
from jax.sharding import PartitionSpec as P

MESH = pl.DeviceIdType.MESH
NX, NY, NZ = 4, 4, 8
PAIRS = 484
PPAD = 512
BLK = 256
CAP = 128
LISTS = 16
F32, BF16, I32 = jnp.float32, jnp.bfloat16, jnp.int32


class Copy:
    def __init__(self, buf, q, rel, rows, way, deps):
        self.buf, self.q, self.rel, self.rows, self.way, self.deps = buf, q, rel, rows, way, deps
        self.number = None

    def arriving(self):
        first, second = self.rel
        if self.way == "s":
            return (first, 1 - second)
        axis, step = self.way[0], 1 if self.way[1] == "+" else -1
        if axis in "xz":
            return (first - step, second)
        return (first, second - step)


def plane_copies(q):
    copies = []

    def add(*args):
        copies.append(Copy("x", q, *args))
        return copies[-1]

    for half, (f, g) in enumerate((("x", "y"), ("y", "x"))):
        base = half * 128
        rows, low, high = (base, 128), (base, 64), (base + 64, 64)

        def at(df, dg, f=f):
            return (df, dg) if f == "x" else (dg, df)

        own_f = [add(at(0, 0), rows, f + s, [("own", q)]) for s in "+-"]
        minus, plus = own_f
        spread = [(0, [("own", q)])]
        fwd = [add(at(-1, 0), low, f + "+", [minus]), add(at(1, 0), high, f + "-", [plus])]
        spread += [(-1, [minus]), (1, [plus]), (2, fwd)]
        for d, deps in spread:
            up = add(at(d, 0), rows, g + "+", deps)
            down = add(at(d, 0), rows, g + "-", deps)
            add(at(d, -1), low, g + "+", [up])
            add(at(d, 1), high, g + "-", [down])
    return copies


def ring_copies(q):
    copies = []

    def add(*args):
        copies.append(Copy("z", q, *args))
        return copies[-1]

    whole = (0, 256)
    have = {0: [("own", q)]}
    add((0, 0), whole, "s", [("own", q)])
    last = {}
    for half in range(2):
        rows = (half * 128, 128)
        for s, sign in (("+", -1), ("-", 1)):
            dep = [("own", q)]
            for t in range(3):
                copy = add((sign * t, 0), rows, "z" + s, dep)
                dep = [copy]
                have.setdefault(sign * (t + 1), []).append(copy)
            last[(half, s)] = dep
    far = [add((-3, 0), (0, 128), "z+", last[(0, "+")]), add((3, 0), (128, 128), "z-", last[(1, "-")])]
    have[4] = far
    for d in (-1, 1, -2, 2, -3, 3, 4):
        add((d, 0), whole, "s", have[d])
    return copies


RATE = {"x": 46.0, "y": 46.0, "z": 46.0, "s": 150.0}
HOP = 1.8


def simulate(copies, own_time):
    ready_at = {}
    free = {}
    arrivals = {}
    pending = list(copies)
    order = []
    while pending:
        best = None
        for copy in pending:
            t = 0.0
            for dep in copy.deps:
                when = own_time[dep[1]] if isinstance(dep, tuple) else arrivals.get(dep.number)
                if when is None:
                    t = None
                    break
                t = max(t, when)
            if t is None:
                continue
            if best is None or (t, copy.number) < best[:2]:
                best = (t, copy.number, copy)
        t, _, copy = best
        start = max(t, free.get(copy.way, 0.0))
        lasting = copy.rows[1] * BLK * 4 / RATE[copy.way[0]] / 1e3
        free[copy.way] = start + lasting
        arrivals[copy.number] = start + lasting + HOP
        order.append(copy.number)
        pending.remove(copy)
    return arrivals, order


J_US, T_US, LEAD_US = 0.7, 0.45, 3.0
N_J, N_T = 16, 32


def make_plan():
    copies = plane_copies(0) + ring_copies(0) + plane_copies(1) + ring_copies(1)
    for n, copy in enumerate(copies):
        copy.number = n
    done_t = LEAD_US + N_J * J_US + N_T * T_US
    arrivals, _ = simulate(copies, {0: 0.0, 1: done_t})
    events = sorted(copies, key=lambda c: (arrivals[c.number], c.number))
    complete = {}
    for copy in copies:
        key = (copy.buf, copy.q, norm(copy.buf, copy.arriving()))
        complete[key] = max(complete.get(key, 0.0), arrivals[copy.number])
    steps = []
    for buf, mod in (("x", None), ("z", None)):
        rels = plane_rels() if buf == "x" else ring_rels()
        for rel in rels:
            ready = complete.get((buf, 1, rel), done_t)
            steps.append((ready, buf, rel))
    steps.sort(key=lambda s: (s[0], s[1], s[2]))
    return copies, arrivals, events, steps, done_t


def norm(buf, rel):
    if buf == "x":
        return (rel[0] % NX, rel[1] % NY)
    return (rel[0] % NZ, rel[1])


def plane_rels():
    return [(i, j) for i in range(NX) for j in range(NY)]


def ring_rels():
    return [(i, j) for i in range(NZ) for j in range(2)]


def split(v):
    high = v.astype(BF16)
    return high, (v - high.astype(F32)).astype(BF16)


def one_hot_rows(index_row, rows, weight=None):
    hit = lax.broadcasted_iota(I32, (rows, index_row.shape[1]), 0) == index_row
    value = 1.0 if weight is None else weight
    return jnp.where(hit, value, 0.0).astype(BF16)


def slot_of(target):
    return (target * 4333) >> 21


def kernel(
    plan,
    shift_ref, c_ref, diag_ref, int_ref,
    src_r, tgt_r, ph_r, src_c, tgt_c, ph_c,
    sigma_ref, corr_ref,
    gx, gz, ipad, ihl, own, oth, jmat, amat, tcol, tacc, acc,
    send_sem, recv_sem, list_send, list_recv,
):
    copies, arrivals, events, steps, done_t = plan
    r, c = lax.axis_index("row"), lax.axis_index("col")
    x, y = r // NY, lax.rem(r, NY)
    z, k = c // 2, lax.rem(c, 2)

    def row_at(dx, dy):
        return lax.rem(x + (dx + NX) % NX, NX) * NY + lax.rem(y + (dy + NY) % NY, NY)

    def col_at(dz, flip):
        return lax.rem(z + (dz + NZ) % NZ, NZ) * 2 + (lax.rem(k + 1, 2) if flip else k)

    def place(buf, rel):
        return row_at(*rel) if buf == "x" else col_at(*rel)

    def device(way):
        if way == "s":
            return (r, col_at(0, 1))
        d = 1 if way[1] == "+" else -1
        if way[0] == "x":
            return (row_at(d, 0), c)
        if way[0] == "y":
            return (row_at(0, d), c)
        return (r, col_at(d, 0))

    bufs = {"x": gx, "z": gz}

    def describe(copy, rel):
        where = bufs[copy.buf].at[copy.q, place(copy.buf, rel), pl.ds(*copy.rows)]
        return pltpu.make_async_remote_copy(
            src_ref=where, dst_ref=where,
            send_sem=send_sem.at[copy.number], recv_sem=recv_sem.at[copy.number],
            device_id=device(copy.way), device_id_type=MESH,
        )

    arrived = set()
    started = set()

    def start_ready():
        for copy in copies:
            if copy.number in started:
                continue
            if all((dep if isinstance(dep, tuple) else dep.number) in arrived for dep in copy.deps):
                started.add(copy.number)
                describe(copy, copy.rel).start()

    def take(copy):
        describe(copy, copy.arriving()).wait_recv()
        arrived.add(copy.number)
        start_ready()

    queue = list(events)

    def pop_until(t):
        out = []
        while queue and arrivals[queue[0].number] <= t:
            out.append(queue.pop(0))
        return out

    barrier = pltpu.get_barrier_semaphore()
    others = ["x+", "x-", "y+", "y-", "z+", "z-", "s"]
    partner = (c, r)
    for way in others:
        pl.semaphore_signal(barrier, inc=1, device_id=device(way), device_id_type=MESH)

    @pl.when(r != c)
    def _():
        pl.semaphore_signal(barrier, inc=1, device_id=partner, device_id_type=MESH)

    gx[0, r] = c_ref[...]
    gz[0, c] = c_ref[...]

    @pl.when(r != c)
    def _():
        pl.semaphore_wait(barrier, len(others) + 1)

    @pl.when(r == c)
    def _():
        pl.semaphore_wait(barrier, len(others))

    lists = (src_r, tgt_r, ph_r, src_c, tgt_c, ph_c)

    def list_copy(n):
        return pltpu.make_async_remote_copy(
            src_ref=lists[n], dst_ref=oth.at[n // 3, n % 3],
            send_sem=list_send.at[n], recv_sem=list_recv.at[n],
            device_id=partner, device_id_type=MESH,
        )

    @pl.when(r != c)
    def _():
        for n in range(6):
            list_copy(n).start()

    arrived.add(("own", 0))
    start_ready()

    for n in range(6):
        own[n // 3, n % 3] = lists[n][...]
    ipad[...] = jnp.zeros_like(ipad)
    ipad[0:PAIRS, 0:PAIRS] = int_ref[...]
    high, low = split(ipad[...].T)
    ihl[0:PPAD, :] = high
    ihl[PPAD:, :] = low
    tacc[...] = jnp.zeros_like(tacc)

    slots_j = {}
    for n in range(N_J):
        slots_j[n] = pop_until(LEAD_US + (n + 1) * J_US)

    def j_step(it, carry):
        side, o0 = it // 8, 2 * lax.rem(it, 8)
        rows = []
        for d in range(2):
            t = own[side, 1, pl.ds(o0 + d, 1), :]
            rows.append(t - PAIRS * slot_of(t))
            hot = one_hot_rows(own[side, 0, pl.ds(o0 + d, 1), :], BLK, own[side, 2, pl.ds(o0 + d, 1), :].astype(F32))
            amat[side, o0 + d, :, 0:CAP] = hot
            amat[side, o0 + d, :, CAP:] = hot
        hot = one_hot_rows(jnp.concatenate(rows, axis=1), PPAD)
        for part in range(2):
            prod = jnp.dot(ihl[pl.ds(part * PPAD, PPAD), :], hot, preferred_element_type=F32).astype(BF16)
            for d in range(2):
                jmat[side, o0 + d, :, part * CAP:(part + 1) * CAP] = prod[:, d * CAP:(d + 1) * CAP]
        for n, evs in slots_j.items():
            if evs:
                @pl.when(it == n)
                def _(evs=evs):
                    for copy in evs:
                        take(copy)
        return carry

    lax.fori_loop(0, N_J, j_step, 0)

    @pl.when(r != c)
    def _():
        for n in range(6):
            list_copy(n).wait()

    @pl.when(r == c)
    def _():
        for n in range(6):
            oth[n // 3, n % 3] = lists[n][...]

    for side in range(2):
        t = jnp.concatenate([oth[side, 1].astype(F32), jnp.zeros((CAP - LISTS, CAP), F32)], axis=0).T.astype(I32)
        for o in range(LISTS):
            tcol[side, o] = jnp.broadcast_to(t[:, o:o + 1], (CAP, CAP))

    slots_t = {}
    for n in range(N_T):
        slots_t[n] = pop_until(LEAD_US + N_J * J_US + (n + 1) * T_US)

    def t_step(it, carry):
        side, o = it // 16, lax.rem(it, 16)
        t = tcol[side, o]
        kc = slot_of(t)
        pc = t - PAIRS * kc
        lane = lax.broadcasted_iota(I32, (CAP, CAP), 1)
        hot = jnp.concatenate(
            [jnp.where(pc - CAP * m == lane, 1.0, 0.0).astype(BF16) for m in range(PPAD // CAP)], axis=1
        )
        g = jnp.dot(hot, jmat[side, o], preferred_element_type=F32)
        same = kc == slot_of(own[side, 1, pl.ds(o, 1), :])
        w = jnp.concatenate(
            [jnp.where(same, g[:, 0:CAP], 0.0).astype(BF16), jnp.where(same, g[:, CAP:], 0.0).astype(BF16)], axis=1
        )
        u = lax.dot_general(w, amat[side, o], (((1,), (1,)), ((), ())), preferred_element_type=F32)
        uh, ul = split(u)
        hot = one_hot_rows(oth[side, 0, pl.ds(o, 1), :], BLK, oth[side, 2, pl.ds(o, 1), :].astype(F32))
        tacc[side] += jnp.dot(
            jnp.concatenate([hot, hot], axis=1), jnp.concatenate([uh, ul], axis=0), preferred_element_type=F32
        )
        for n, evs in slots_t.items():
            if evs:
                @pl.when(it == n)
                def _(evs=evs):
                    for copy in evs:
                        take(copy)
        return carry

    lax.fori_loop(0, N_T, t_step, 0)

    gz[1, c] = tacc[0].T
    gx[1, r] = tacc[1]
    arrived.add(("own", 1))
    start_ready()
    for copy in [e for e in queue if e.q == 0]:
        take(copy)
    queue[:] = [e for e in queue if e.q == 1]

    acc[...] = jnp.zeros_like(acc)
    slots_f = {}
    for n, (ready, buf, rel) in enumerate(steps):
        slots_f[n] = pop_until(ready if n < len(steps) - 1 else 1e9)

    def f_step(it, carry):
        for n, evs in slots_f.items():
            if evs:
                @pl.when(it == n)
                def _(evs=evs):
                    for copy in evs:
                        take(copy)
        index = 0
        which = 0
        for n, (_, buf, rel) in enumerate(steps):
            index = jnp.where(it == n, place(buf, rel), index)
            which = jnp.where(it == n, 1 if buf == "x" else 0, which)
        left_high, left_low = split(gz[1 - which, index])
        right_high, right_low = split(gx[which, index])
        acc[...] += jnp.dot(
            jnp.concatenate([left_high, left_high, left_low], axis=1),
            jnp.concatenate([right_high, right_low, right_high], axis=0),
            preferred_element_type=F32,
        )
        return carry

    lax.fori_loop(0, len(steps), f_step, 0)

    sigma = acc[...]
    sigma_ref[...] = sigma
    shift = shift_ref[0]
    corr_ref[...] = (sigma - shift * c_ref[...]) / (diag_ref[...] - shift)

    for copy in copies:
        describe(copy, copy.rel).wait_send()


def shards(coefficients, diagonal, energy_shift, integrals, source_row, target_row, phase_row,
           source_col, target_col, phase_col):
    plan = make_plan()
    n_copies = len(plan[0])
    vmem = pl.BlockSpec(memory_space=pltpu.VMEM)
    out = jax.ShapeDtypeStruct((BLK, BLK), F32)
    return pl.pallas_call(
        functools.partial(kernel, plan),
        out_shape=(out, out),
        in_specs=[pl.BlockSpec(memory_space=pltpu.SMEM)] + [vmem] * 9,
        out_specs=(vmem, vmem),
        scratch_shapes=[
            pltpu.VMEM((2, 16, BLK, BLK), F32),
            pltpu.VMEM((2, 16, BLK, BLK), F32),
            pltpu.VMEM((PPAD, PPAD), F32),
            pltpu.VMEM((2 * PPAD, PPAD), BF16),
            pltpu.VMEM((2, 3, LISTS, CAP), I32),
            pltpu.VMEM((2, 3, LISTS, CAP), I32),
            pltpu.VMEM((2, LISTS, PPAD, 2 * CAP), BF16),
            pltpu.VMEM((2, LISTS, BLK, 2 * CAP), BF16),
            pltpu.VMEM((2, LISTS, CAP, CAP), I32),
            pltpu.VMEM((2, BLK, BLK), F32),
            pltpu.VMEM((BLK, BLK), F32),
            pltpu.SemaphoreType.DMA((n_copies,)),
            pltpu.SemaphoreType.DMA((n_copies,)),
            pltpu.SemaphoreType.DMA((6,)),
            pltpu.SemaphoreType.DMA((6,)),
        ],
        compiler_params=pltpu.CompilerParams(
            collective_id=0, has_side_effects=True, vmem_limit_bytes=60 * 1024 * 1024
        ),
    )(energy_shift, coefficients, diagonal, integrals, source_row, target_row, phase_row,
      source_col, target_col, phase_col)


def solution(mesh):
    in_specs = (
        P("row", "col"),
        P("row", "col"),
        P(),
        P(),
        P("row", None),
        P("row", None),
        P("row", None),
        P("col", None),
        P("col", None),
        P("col", None),
    )
    out_specs = (P("row", "col"), P("row", "col"))
    return jax.shard_map(shards, mesh=mesh, in_specs=in_specs, out_specs=out_specs, check_vma=False)
```

time: 362 us -> 95.2 us (0.26)
  waiting for transfers between devices: 130 us -> 0 us
  other arithmetic: 96 us -> 0 us
  Pallas kernels: 0 us -> 91.4 us
  local copies, waits for them, and re-layouts: 50.3 us -> 2.42 us
  starting transfers between devices: 35.3 us -> 0 us
  matrix products: 32.7 us -> 0 us
  between operations: 14.9 us -> 1.3 us
    pallas_call x0 -> x1, Pallas kernels: none -> 91.4 us  [shards(): pl.pallas_call(functools.partial(kernel, plan), out_shape=(out, out), in_...]
    scatter-add x4 -> x0, other arithmetic: 84.9 us -> none  [the longest x2 54.5 us: local_terms(): return jnp.zeros((row_count, lane_count), jnp.float32).at[jnp.clip(offset...]
    all_to_all x4 -> x0, waiting for transfers between devices: 74.3 us -> none  [the longest x1 48.7 us: beta_sigma(): lax.all_to_all(signed_rows(block, source, phases), 'col', split_axis=0, c...]
    reduce_scatter x2 -> x0, waiting for transfers between devices: 55.5 us -> none  [the longest x1 55.4 us: beta_sigma(): lax.psum_scatter(local_terms(picked, meta_in, jnp.int32(0), lax.axis_size...]
    all_to_all x4 -> x0, starting transfers between devices: 35 us -> none  [the longest x1 13.6 us: beta_sigma(): lax.all_to_all(entry_meta, 'col', split_axis=0, concat_axis=0, tiled=True)]
    dot_general x2 -> x0, matrix products: 32.7 us -> none  [owner_products(): jnp.einsum('ip,kpb->kib', integrals, densities.reshape(-1, pair_count, la...]
    reshape x4 -> x0, local copies, waits for them, and re-layouts: 27.7 us -> none  [the longest x2 13.9 us: owner_products(): products = jnp.einsum('ip,kpb->kib', integrals, densities.reshape(-1, pai...]
    gather x2 -> x0, local copies, waits for them, and re-layouts: 16.2 us -> none  [signed_rows(): return block[source] * phases[..., None].astype(jnp.float32)]
  transfers between devices with their start and end apart: 6 -> 0, of which waited for: 3 -> 0; matrix products, arithmetic and copies ran while one was open for 28% -> 0% of each run, Pallas kernels for 0% -> 0%
where the time goes in v1:
time: 95.2 us; the launch traced here: 95.1 us
  Pallas kernels  91.4 us (96%)
  local copies, waits for them, and re-layouts  2.42 us (3%)
  between operations  1.3 us (1%)
    pallas_call x1, Pallas kernels, shards(): pl.pallas_call(functools.partial(kernel, plan), out_shape=(out, out), in_...  91.4 us
    unnamed x4, local copies, waits for them, and re-layouts  2.42 us

profile of v1, /device:TPU:1, one launch (start us, length us, event | category | flops | bytes accessed | tf_op | source)
XLA Modules:
  0.0 95.1 jit_solution(3412154953417513319)
XLA Ops:
  1.3 91.4 %shard_map.113 = (f32[256,256]{1,0:T(8,128)}, f32[256,256]{1,0:T(8,128)}) custom-call(f32[1]{0:T(128)S(6)} %copy.14.shift_ref, f32[256,256]{1,0:T(8,128)} %c_ref.1, f32[256,256]{1,0:T(8,128)} %diag_ref.1, f32[484,484]{1,0:T(8,128)} %int_ref.1, s32[16,128]{1,0:T(8,128)} %src_r.1, s32[16,128]{1,0:T(8,128)} %tgt_r.1, s32[16,128]{1,0:T(8,128)} %ph_r.1, ...), custom_call_target="tpu_custom_call" | custom-call | tf_op jit(solution)/shard_map/pallas_call | solution.py:418
  92.6 0.0 copy-start
  92.7 1.7 %copy.15 = f32[256,256]{1,0:T(8,128)} copy(f32[256,256]{1,0:T(8,128)} %get-tuple-element.4) | data formatting | bytes 524288
  94.4 0.0 copy-done
  94.4 0.7 copy.16
Async XLA Ops:
  92.6 1.7 %copy-start = (f32[256,256]{1,0:T(8,128)S(1)}, f32[256,256]{1,0:T(8,128)}, u32[]{:S(2)}) copy-start(f32[256,256]{1,0:T(8,128)} %get-tuple-element.5) | copy-start | bytes 786436

commit v2 on v1

v2 whole, which is shorter than its diff:
```python
import functools

import jax
import jax.numpy as jnp
from jax import lax
from jax.experimental import pallas as pl
from jax.experimental.pallas import tpu as pltpu
from jax.sharding import PartitionSpec as P

MESH = pl.DeviceIdType.MESH
NX, NY, NZ = 4, 4, 8
PAIRS = 484
PPAD = 512
BLK = 256
CAP = 128
LISTS = 16
F32, BF16, I32 = jnp.float32, jnp.bfloat16, jnp.int32


class Copy:
    def __init__(self, buf, q, rel, rows, way, deps):
        self.buf, self.q, self.rel, self.rows, self.way, self.deps = buf, q, rel, rows, way, deps
        self.number = None

    def arriving(self):
        rel = list(self.rel)
        if self.way == "s":
            rel[1] = 1 - rel[1]
        elif self.q == 1:
            rel[0] = 1 - rel[0]
        else:
            step = 1 if self.way[1] == "+" else -1
            rel[0 if self.way[0] in "xz" else 1] -= step
        return tuple(rel)


WHOLE = (0, BLK)


def plane_copies():
    copies = []

    def add(*args):
        copies.append(Copy("x", 0, *args))
        return copies[-1]

    for half, (f, g) in enumerate((("x", "y"), ("y", "x"))):
        base = half * 128
        rows, low, high = (base, 128), (base, 64), (base + 64, 64)

        def at(df, dg, f=f):
            return (df, dg) if f == "x" else (dg, df)

        own_f = [add(at(0, 0), rows, f + s, ["C"]) for s in "+-"]
        minus, plus = own_f
        spread = [(0, ["C"])]
        fwd = [add(at(-1, 0), low, f + "+", [minus]), add(at(1, 0), high, f + "-", [plus])]
        spread += [(-1, [minus]), (1, [plus]), (2, fwd)]
        for d, deps in spread:
            up = add(at(d, 0), rows, g + "+", deps)
            down = add(at(d, 0), rows, g + "-", deps)
            add(at(d, -1), low, g + "+", [up])
            add(at(d, 1), high, g + "-", [down])
    return copies


def ring_copies():
    copies = []

    def add(*args):
        copies.append(Copy("z", 0, *args))
        return copies[-1]

    have = {}
    add((0, 0), WHOLE, "s", ["C"])
    last = {}
    for half in range(2):
        rows = (half * 128, 128)
        for s, sign in (("+", -1), ("-", 1)):
            dep = ["C"]
            for t in range(3):
                copy = add((sign * t, 0), rows, "z" + s, dep)
                dep = [copy]
                have.setdefault(sign * (t + 1), []).append(copy)
            last[(half, s)] = dep
    have[4] = [add((-3, 0), (0, 128), "z+", last[(0, "+")]), add((3, 0), (128, 128), "z-", last[(1, "-")])]
    for d in (-1, 1, -2, 2, -3, 3, 4):
        add((d, 0), WHOLE, "s", have[d])
    return copies, {"z+": last[(0, "+")] + last[(1, "+")], "z-": last[(0, "-")] + last[(1, "-")]}


def block_copies(last):
    copies = []
    for j in range(GROUP):
        way = "z+" if j % 2 == 0 else "z-"
        far = Copy("z", 1, (0, 0, j), WHOLE, way, ["T0"] + last[way])
        copies += [far, Copy("z", 1, (0, 0, j), WHOLE, "s", ["T0"]), Copy("z", 1, (1, 0, j), WHOLE, "s", [far])]
    for j in range(2 * GROUP):
        way = ("x+", "x-", "y+", "y-")[j % 4]
        copies.append(Copy("x", 1, (0, j), WHOLE, way, ["T%d" % (1 + j // GROUP)]))
    return copies


RATE = {"x": 46.8, "y": 46.8, "z": 46.8, "s": 350.0}
HOP = 1.8


def simulate(copies, own_time):
    free, arrivals, pending = {}, {}, list(copies)
    while pending:
        best = None
        for copy in pending:
            times = [own_time[dep] if isinstance(dep, str) else arrivals.get(dep.number) for dep in copy.deps]
            if None in times:
                continue
            if best is None or (max(times), copy.number) < best[:2]:
                best = (max(times), copy.number, copy)
        t, _, copy = best
        start = max(t, free.get(copy.way, 0.0))
        lasting = copy.rows[1] * BLK * 4 / RATE[copy.way[0]] / 1e3
        free[copy.way] = start + lasting
        arrivals[copy.number] = start + lasting + HOP
        pending.remove(copy)
    return arrivals


GROUP = 4
PHASES = 3
N_J, J_US = 8, 0.8
N_T, T_US = 16 * PHASES, 0.5
LIST_US = 5.0
T0_US = N_J * J_US + 2.5


def make_plan():
    ring, last = ring_copies()
    copies = plane_copies() + ring + block_copies(last)
    for n, copy in enumerate(copies):
        copy.number = n
    own_time = {"C": 0.0}
    for p in range(PHASES):
        own_time["T%d" % p] = T0_US + (p + 1) * 16 * T_US
    arrivals = simulate(copies, own_time)
    events = sorted(copies, key=lambda c: (arrivals[c.number], c.number))
    ready = {}
    for copy in copies:
        if copy.q == 1:
            ready[(copy.buf, copy.arriving())] = arrivals[copy.number]
    steps = []
    for j in range(GROUP):
        steps.append((own_time["T0"], "z", (0, 0, j)))
    for j in range(2 * GROUP):
        steps.append((own_time["T%d" % (1 + j // GROUP)], "x", (0, j)))
    steps += [(when, buf, rel) for (buf, rel), when in ready.items()]
    steps.sort(key=lambda s: (s[0], s[1], s[2]))
    return copies, arrivals, events, steps


def split(v):
    high = v.astype(BF16)
    return high, (v - high.astype(F32)).astype(BF16)


def one_hot_rows(index_row, rows, weight=None):
    hit = lax.broadcasted_iota(I32, (rows, index_row.shape[1]), 0) == index_row
    value = 1.0 if weight is None else weight
    return jnp.where(hit, value, 0.0).astype(BF16)


def slot_of(target):
    return (target * 4333) >> 21


def kernel(
    plan,
    shift_ref, c_ref, diag_ref, int_ref,
    src_r, tgt_r, ph_r, src_c, tgt_c, ph_c,
    sigma_ref, corr_ref,
    gx, gz, ints, diag, ipad, ihl, own, oth, jmat, amat, tcol, tacc, acc,
    load_sem, send_sem, recv_sem, a_send, a_recv, b_send, b_recv, f_send,
):
    copies, arrivals, events, steps = plan
    r, c = lax.axis_index("row"), lax.axis_index("col")
    x, y = r // NY, lax.rem(r, NY)
    z, k = c // 2, lax.rem(c, 2)
    zpar, xpar = lax.rem(z, 2), lax.rem(x + y, 2)

    def flip(v, by):
        return 1 - v if by else v

    def row_at(dx, dy):
        return lax.rem(x + (dx + NX) % NX, NX) * NY + lax.rem(y + (dy + NY) % NY, NY)

    def col_at(dz, by):
        return lax.rem(z + (dz + NZ) % NZ, NZ) * 2 + flip(k, by)

    def place(buf, q, rel):
        if q == 0:
            return row_at(*rel) if buf == "x" else col_at(*rel)
        if buf == "x":
            return 2 * GROUP * flip(xpar, rel[0]) + rel[1]
        return 2 * GROUP * flip(zpar, rel[0]) + GROUP * flip(k, rel[1]) + rel[2]

    def device(way):
        if way == "s":
            return (r, col_at(0, 1))
        d = 1 if way[1] == "+" else -1
        if way[0] == "x":
            return (row_at(d, 0), c)
        if way[0] == "y":
            return (row_at(0, d), c)
        return (r, col_at(d, 0))

    bufs = {"x": gx, "z": gz}

    def describe(copy, rel):
        where = bufs[copy.buf].at[copy.q, place(copy.buf, copy.q, rel), pl.ds(*copy.rows)]
        return pltpu.make_async_remote_copy(
            src_ref=where, dst_ref=where,
            send_sem=send_sem.at[copy.number], recv_sem=recv_sem.at[copy.number],
            device_id=device(copy.way), device_id_type=MESH,
        )

    arrived, started = set(), set()

    def start_ready():
        for copy in copies:
            if copy.number in started:
                continue
            if all((dep if isinstance(dep, str) else dep.number) in arrived for dep in copy.deps):
                started.add(copy.number)
                describe(copy, copy.rel).start()

    def have(name):
        arrived.add(name)
        start_ready()

    def take(copy):
        describe(copy, copy.arriving()).wait_recv()
        have(copy.number)

    queue = list(events)

    def pop_until(t):
        out = []
        while queue and arrivals[queue[0].number] <= t:
            out.append(queue.pop(0))
        return out

    def at_step(it, slots):
        for n, evs in slots.items():
            if evs:
                @pl.when(it == n)
                def _(evs=evs):
                    for copy in evs:
                        if callable(copy):
                            copy()
                        else:
                            take(copy)

    lists = (src_r, tgt_r, ph_r, src_c, tgt_c, ph_c)
    loads = [pltpu.make_async_copy(lists[n], own.at[n // 3, n % 3], load_sem.at[n]) for n in range(6)]
    loads.append(pltpu.make_async_copy(c_ref, gx.at[0, r], load_sem.at[6]))
    loads.append(pltpu.make_async_copy(c_ref, gz.at[0, c], load_sem.at[7]))
    loads.append(pltpu.make_async_copy(int_ref, ints, load_sem.at[8]))
    loads.append(pltpu.make_async_copy(diag_ref, diag, load_sem.at[9]))
    for load in loads:
        load.start()

    plane = [(dx, dy) for dx in range(NX) for dy in range(NY) if (dx, dy) != (0, 0)]
    peers = [(row_at(*rel), c) for rel in plane] + [(r, col_at(d, 0)) for d in range(1, NZ)] + [(r, col_at(0, 1))]
    barrier = pltpu.get_barrier_semaphore()
    for peer in peers:
        pl.semaphore_signal(barrier, inc=1, device_id=peer, device_id_type=MESH)
    for load in loads[:8]:
        load.wait()
    pl.semaphore_wait(barrier, len(peers))

    ax = 2 * zpar + k
    bz = (NZ // 2) * xpar
    in_a = x == ax
    in_b = z // (NZ // 2) == xpar

    def a_copy(n, slot):
        return pltpu.make_async_remote_copy(
            src_ref=own.at[0], dst_ref=oth.at[slot], send_sem=a_send.at[n], recv_sem=a_recv.at[slot],
            device_id=(row_at(*plane[n]), c), device_id_type=MESH,
        )

    def b_copy(n, jz):
        return pltpu.make_async_remote_copy(
            src_ref=own.at[1], dst_ref=oth.at[GROUP + 2 * jz + k], send_sem=b_send.at[n],
            recv_sem=b_recv.at[2 * jz + k],
            device_id=(r, col_at(n + 1, 0)), device_id_type=MESH,
        )

    def f_copy(jz, core, mine):
        slot = 2 * jz + core
        return pltpu.make_async_remote_copy(
            src_ref=own.at[1] if mine else oth.at[GROUP + slot], dst_ref=oth.at[GROUP + slot],
            send_sem=f_send.at[jz], recv_sem=b_recv.at[slot],
            device_id=(r, col_at(0, 1)), device_id_type=MESH,
        )

    @pl.when(in_b)
    def _():
        for n in range(NZ - 1):
            b_copy(n, z - bz).start()

    @pl.when(in_a)
    def _():
        for n in range(len(plane)):
            a_copy(n, y).start()

    have("C")

    def forward_lists():
        for jz in range(NZ // 2):
            @pl.when(z == bz + jz)
            def _(jz=jz):
                f_copy(jz, k, True).start()

            @pl.when(z != bz + jz)
            def _(jz=jz):
                b_copy(0, jz).wait_recv()
                f_copy(jz, k, False).start()

    ipad[...] = jnp.zeros_like(ipad)
    loads[8].wait()
    ipad[0:PAIRS, 0:PAIRS] = ints[...]
    high, low = split(ipad[...].T)
    ihl[0:PPAD, :] = high
    ihl[PPAD:, :] = low
    tacc[...] = jnp.zeros_like(tacc)

    slots_j = {n: pop_until((n + 1) * J_US) for n in range(N_J)}
    slots_j[min(N_J - 1, int(LIST_US / J_US))].append(forward_lists)

    def j_step(it, carry):
        side, o0 = it // (N_J // 2), 4 * lax.rem(it, N_J // 2)
        rows = []
        for d in range(4):
            t = own[side, 1, pl.ds(o0 + d, 1), :]
            rows.append(t - PAIRS * slot_of(t))
            hot = one_hot_rows(own[side, 0, pl.ds(o0 + d, 1), :], BLK, own[side, 2, pl.ds(o0 + d, 1), :].astype(F32))
            amat[side, o0 + d, :, 0:CAP] = hot
            amat[side, o0 + d, :, CAP:] = hot
        hot = one_hot_rows(jnp.concatenate(rows, axis=1), PPAD)
        for part in range(2):
            prod = jnp.dot(ihl[pl.ds(part * PPAD, PPAD), :], hot, preferred_element_type=F32).astype(BF16)
            for d in range(4):
                jmat[side, o0 + d, :, part * CAP:(part + 1) * CAP] = prod[:, d * CAP:(d + 1) * CAP]
        at_step(it, slots_j)
        return carry

    lax.fori_loop(0, N_J, j_step, 0)

    for j in range(GROUP):
        @pl.when(jnp.logical_not(in_a & (y == j)))
        def _(j=j):
            a_copy(0, j).wait_recv()
    for jz in range(NZ // 2):
        f_copy(jz, 1 - k, False).wait_recv()

    @pl.when(in_a)
    def _():
        oth[y] = own[0]

    @pl.when(in_b)
    def _():
        oth[GROUP + 2 * (z - bz) + k] = own[1]

    def turn(b, carry):
        t = jnp.concatenate([oth[b, 1].astype(F32), jnp.zeros((CAP - LISTS, CAP), F32)], axis=0).T.astype(I32)
        for o in range(LISTS):
            tcol[b, o] = jnp.broadcast_to(t[:, o:o + 1], (CAP, CAP))
        return carry

    lax.fori_loop(0, GROUP * PHASES, turn, 0)

    slots_t = {n: pop_until(T0_US + (n + 1) * T_US) for n in range(N_T)}

    def finish(p):
        def act():
            for j in range(GROUP):
                if p == 0:
                    gz[1, place("z", 1, (0, 0, j))] = tacc[j].T
                else:
                    gx[1, place("x", 1, (0, GROUP * (p - 1) + j))] = tacc[GROUP * p + j]
            have("T%d" % p)
        return act

    for p in range(PHASES):
        slots_t[16 * p + 15].insert(0, finish(p))

    def t_step(it, carry):
        p, o = it // 16, lax.rem(it, 16)
        side = jnp.minimum(p, 1)
        lane = lax.broadcasted_iota(I32, (CAP, CAP), 1)
        slots, hots = [], []
        for j in range(GROUP):
            t = tcol[GROUP * p + j, o]
            kc = slot_of(t)
            pc = t - PAIRS * kc
            slots.append(kc)
            hots.append(jnp.concatenate(
                [jnp.where(pc - CAP * m == lane, 1.0, 0.0).astype(BF16) for m in range(PPAD // CAP)], axis=1
            ))
        g = jnp.dot(jnp.concatenate(hots, axis=0), jmat[side, o], preferred_element_type=F32)
        mine = slot_of(own[side, 1, pl.ds(o, 1), :])
        ws = []
        for j in range(GROUP):
            same = slots[j] == mine
            part = g[CAP * j:CAP * (j + 1)]
            ws.append(jnp.concatenate(
                [jnp.where(same, part[:, 0:CAP], 0.0).astype(BF16), jnp.where(same, part[:, CAP:], 0.0).astype(BF16)],
                axis=1,
            ))
        u = lax.dot_general(
            jnp.concatenate(ws, axis=0), amat[side, o], (((1,), (1,)), ((), ())), preferred_element_type=F32
        )
        for j in range(GROUP):
            b = GROUP * p + j
            uh, ul = split(u[CAP * j:CAP * (j + 1)])
            hot = one_hot_rows(oth[b, 0, pl.ds(o, 1), :], BLK, oth[b, 2, pl.ds(o, 1), :].astype(F32))
            tacc[b] += jnp.dot(
                jnp.concatenate([hot, hot], axis=1), jnp.concatenate([uh, ul], axis=0), preferred_element_type=F32
            )
        at_step(it, slots_t)
        return carry

    lax.fori_loop(0, N_T, t_step, 0)

    for copy in [e for e in queue if e.q == 0]:
        take(copy)
    queue[:] = [e for e in queue if e.q == 1]

    acc[...] = jnp.zeros_like(acc)
    n_f = len(steps) // 2
    slots_f = {n: pop_until(steps[2 * n + 1][0] if n < n_f - 1 else 1e9) for n in range(n_f)}

    def f_step(it, carry):
        at_step(it, slots_f)
        lefts, rights = [], []
        for d in range(2):
            index, which = 0, 0
            for n in range(n_f):
                _, buf, rel = steps[2 * n + d]
                index = jnp.where(it == n, place(buf, 1, rel), index)
                which = jnp.where(it == n, 1 if buf == "x" else 0, which)
            left_high, left_low = split(gz[1 - which, index])
            right_high, right_low = split(gx[which, index])
            lefts += [left_high, left_high, left_low]
            rights += [right_high, right_low, right_high]
        acc[...] += jnp.dot(
            jnp.concatenate(lefts, axis=1), jnp.concatenate(rights, axis=0), preferred_element_type=F32
        )
        return carry

    lax.fori_loop(0, n_f, f_step, 0)

    sigma = acc[...]
    sigma_ref[...] = sigma
    shift = shift_ref[0]
    loads[9].wait()
    corr_ref[...] = (sigma - shift * gx[0, r]) / (diag[...] - shift)

    for copy in copies:
        describe(copy, copy.rel).wait_send()

    @pl.when(in_b)
    def _():
        for n in range(NZ - 1):
            b_copy(n, z - bz).wait_send()

    @pl.when(in_a)
    def _():
        for n in range(len(plane)):
            a_copy(n, y).wait_send()

    for jz in range(NZ // 2):
        f_copy(jz, k, False).wait_send()


def shards(coefficients, diagonal, energy_shift, integrals, source_row, target_row, phase_row,
           source_col, target_col, phase_col):
    plan = make_plan()
    n_copies = len(plan[0])
    vmem = pl.BlockSpec(memory_space=pltpu.VMEM)
    out = jax.ShapeDtypeStruct((BLK, BLK), F32)
    blocks = GROUP * PHASES
    return pl.pallas_call(
        functools.partial(kernel, plan),
        out_shape=(out, out),
        in_specs=[pl.BlockSpec(memory_space=pltpu.SMEM)] + [pl.BlockSpec(memory_space=pl.ANY)] * 9,
        out_specs=(vmem, vmem),
        scratch_shapes=[
            pltpu.VMEM((2, 16, BLK, BLK), F32),
            pltpu.VMEM((2, 16, BLK, BLK), F32),
            pltpu.VMEM((PAIRS, PAIRS), F32),
            pltpu.VMEM((BLK, BLK), F32),
            pltpu.VMEM((PPAD, PPAD), F32),
            pltpu.VMEM((2 * PPAD, PPAD), BF16),
            pltpu.VMEM((2, 3, LISTS, CAP), I32),
            pltpu.VMEM((blocks, 3, LISTS, CAP), I32),
            pltpu.VMEM((2, LISTS, PPAD, 2 * CAP), BF16),
            pltpu.VMEM((2, LISTS, BLK, 2 * CAP), BF16),
            pltpu.VMEM((blocks, LISTS, CAP, CAP), I32),
            pltpu.VMEM((blocks, BLK, BLK), F32),
            pltpu.VMEM((BLK, BLK), F32),
            pltpu.SemaphoreType.DMA((10,)),
            pltpu.SemaphoreType.DMA((n_copies,)),
            pltpu.SemaphoreType.DMA((n_copies,)),
            pltpu.SemaphoreType.DMA((15,)),
            pltpu.SemaphoreType.DMA((GROUP,)),
            pltpu.SemaphoreType.DMA((NZ - 1,)),
            pltpu.SemaphoreType.DMA((2 * GROUP,)),
            pltpu.SemaphoreType.DMA((NZ // 2,)),
        ],
        compiler_params=pltpu.CompilerParams(
            collective_id=0, has_side_effects=True, vmem_limit_bytes=60 * 1024 * 1024
        ),
    )(energy_shift, coefficients, diagonal, integrals, source_row, target_row, phase_row,
      source_col, target_col, phase_col)


def solution(mesh):
    in_specs = (
        P("row", "col"),
        P("row", "col"),
        P(),
        P(),
        P("row", None),
        P("row", None),
        P("row", None),
        P("col", None),
        P("col", None),
        P("col", None),
    )
    out_specs = (P("row", "col"), P("row", "col"))
    return jax.shard_map(shards, mesh=mesh, in_specs=in_specs, out_specs=out_specs, check_vma=False)
```

time: 95.2 us -> 99.7 us (1.047)
  Pallas kernels: 91.4 us -> 95.9 us
    pallas_call x1, Pallas kernels: 91.4 us -> 95.9 us  [shards(): pl.pallas_call(functools.partial(kernel, plan), out_shape=(out, out), in_...]
where the time goes in v2:
time: 99.7 us; the launch traced here: 99.6 us
  Pallas kernels  95.9 us (96%)
  local copies, waits for them, and re-layouts  2.42 us (2%)
  between operations  1.3 us (1%)
    pallas_call x1, Pallas kernels, shards(): pl.pallas_call(functools.partial(kernel, plan), out_shape=(out, out), in_...  95.9 us
    unnamed x4, local copies, waits for them, and re-layouts  2.42 us

profile of v2, /device:TPU:1, one launch (start us, length us, event | category | flops | bytes accessed | tf_op | source)
XLA Modules:
  0.0 99.6 jit_solution(9478817128545967649)
XLA Ops:
  1.3 95.9 %shard_map.113 = (f32[256,256]{1,0:T(8,128)}, f32[256,256]{1,0:T(8,128)}) custom-call(f32[1]{0:T(128)S(6)} %copy.14.shift_ref, f32[256,256]{1,0:T(8,128)} %c_ref.1, f32[256,256]{1,0:T(8,128)} %diag_ref.1, f32[484,484]{1,0:T(8,128)} %int_ref.1, s32[16,128]{1,0:T(8,128)} %src_r.1, s32[16,128]{1,0:T(8,128)} %tgt_r.1, s32[16,128]{1,0:T(8,128)} %ph_r.1, ...), custom_call_target="tpu_custom_call" | custom-call | tf_op jit(solution)/shard_map/pallas_call | solution.py:492
  97.2 0.0 copy-start
  97.2 1.7 %copy.15 = f32[256,256]{1,0:T(8,128)} copy(f32[256,256]{1,0:T(8,128)} %get-tuple-element.4) | data formatting | bytes 524288
  98.9 0.0 copy-done
  98.9 0.7 copy.16
Async XLA Ops:
  97.2 1.7 %copy-start = (f32[256,256]{1,0:T(8,128)S(1)}, f32[256,256]{1,0:T(8,128)}, u32[]{:S(2)}) copy-start(f32[256,256]{1,0:T(8,128)} %get-tuple-element.5) | copy-start | bytes 786436

commit v3 on v2

--- a/solution.py
+++ b/solution.py
@@ -127,9 +127,10 @@
 GROUP = 4
 PHASES = 3
 N_J, J_US = 8, 0.8
-N_T, T_US = 16 * PHASES, 0.5
+ITEMS = 16 * PHASES
+N_T, T_US = ITEMS // 2 + 1, 0.9
 LIST_US = 5.0
-T0_US = N_J * J_US + 2.5
+T0_US = N_J * J_US + 1.5
 
 
 def make_plan():
@@ -139,7 +140,7 @@
         copy.number = n
     own_time = {"C": 0.0}
     for p in range(PHASES):
-        own_time["T%d" % p] = T0_US + (p + 1) * 16 * T_US
+        own_time["T%d" % p] = T0_US + (8 * p + 9) * T_US
     arrivals = simulate(copies, own_time)
     events = sorted(copies, key=lambda c: (arrivals[c.number], c.number))
     ready = {}
@@ -176,7 +177,8 @@
     shift_ref, c_ref, diag_ref, int_ref,
     src_r, tgt_r, ph_r, src_c, tgt_c, ph_c,
     sigma_ref, corr_ref,
-    gx, gz, ints, diag, ipad, ihl, own, oth, jmat, amat, tcol, tacc, acc,
+    gx, gz, ints, diag, ipad, ihl, own, oth, jmat, amat, turned, hot_0, hot_1, slot_0, slot_1, w_0, w_1, u_0, u_1,
+    tacc, acc,
     load_sem, send_sem, recv_sem, a_send, a_recv, b_send, b_recv, f_send,
 ):
     copies, arrivals, events, steps = plan
@@ -312,8 +314,6 @@
         for n in range(len(plane)):
             a_copy(n, y).start()
 
-    have("C")
-
     def forward_lists():
         for jz in range(NZ // 2):
             @pl.when(z == bz + jz)
@@ -331,7 +331,9 @@
     high, low = split(ipad[...].T)
     ihl[0:PPAD, :] = high
     ihl[PPAD:, :] = low
-    tacc[...] = jnp.zeros_like(tacc)
+    have("C")
+    for ref in (tacc, w_0, w_1, u_0, u_1):
+        ref[...] = jnp.zeros_like(ref)
 
     slots_j = {n: pop_until((n + 1) * J_US) for n in range(N_J)}
     slots_j[min(N_J - 1, int(LIST_US / J_US))].append(forward_lists)
@@ -355,30 +357,34 @@
 
     lax.fori_loop(0, N_J, j_step, 0)
 
+    def turn(blocks):
+        for b in blocks:
+            t = jnp.concatenate([oth[b, 1].astype(F32), jnp.zeros((CAP - LISTS, CAP), F32)], axis=0)
+            turned[b] = t.T.astype(I32)
+
     for j in range(GROUP):
         @pl.when(jnp.logical_not(in_a & (y == j)))
         def _(j=j):
             a_copy(0, j).wait_recv()
-    for jz in range(NZ // 2):
-        f_copy(jz, 1 - k, False).wait_recv()
 
     @pl.when(in_a)
     def _():
         oth[y] = own[0]
 
-    @pl.when(in_b)
-    def _():
-        oth[GROUP + 2 * (z - bz) + k] = own[1]
-
-    def turn(b, carry):
-        t = jnp.concatenate([oth[b, 1].astype(F32), jnp.zeros((CAP - LISTS, CAP), F32)], axis=0).T.astype(I32)
-        for o in range(LISTS):
-            tcol[b, o] = jnp.broadcast_to(t[:, o:o + 1], (CAP, CAP))
-        return carry
-
-    lax.fori_loop(0, GROUP * PHASES, turn, 0)
+    turn(range(GROUP))
+
+    def beta_lists():
+        for jz in range(NZ // 2):
+            f_copy(jz, 1 - k, False).wait_recv()
+
+        @pl.when(in_b)
+        def _():
+            oth[GROUP + 2 * (z - bz) + k] = own[1]
+
+        turn(range(GROUP, GROUP * PHASES))
 
     slots_t = {n: pop_until(T0_US + (n + 1) * T_US) for n in range(N_T)}
+    slots_t[5].insert(0, beta_lists)
 
     def finish(p):
         def act():
@@ -391,42 +397,59 @@
         return act
 
     for p in range(PHASES):
-        slots_t[16 * p + 15].insert(0, finish(p))
-
-    def t_step(it, carry):
-        p, o = it // 16, lax.rem(it, 16)
-        side = jnp.minimum(p, 1)
+        slots_t[8 * p + 8].insert(0, finish(p))
+
+    def item_of(item):
+        item = jnp.clip(item, 0, ITEMS - 1)
+        p = item // 16
+        return p, lax.rem(item, 16), jnp.minimum(p, 1)
+
+    def stage_hot(item, hot_ref, slot_ref):
+        p, o, _ = item_of(item)
         lane = lax.broadcasted_iota(I32, (CAP, CAP), 1)
-        slots, hots = [], []
         for j in range(GROUP):
-            t = tcol[GROUP * p + j, o]
+            t = jnp.take_along_axis(turned[GROUP * p + j], jnp.full((CAP, CAP), o, I32), axis=1,
+                                    mode="promise_in_bounds")
             kc = slot_of(t)
             pc = t - PAIRS * kc
-            slots.append(kc)
-            hots.append(jnp.concatenate(
-                [jnp.where(pc - CAP * m == lane, 1.0, 0.0).astype(BF16) for m in range(PPAD // CAP)], axis=1
-            ))
-        g = jnp.dot(jnp.concatenate(hots, axis=0), jmat[side, o], preferred_element_type=F32)
-        mine = slot_of(own[side, 1, pl.ds(o, 1), :])
-        ws = []
+            slot_ref[CAP * j:CAP * (j + 1), :] = kc
+            for m in range(PPAD // CAP):
+                hot = jnp.where(pc == lane + CAP * m, 1.0, 0.0).astype(BF16)
+                hot_ref[CAP * j:CAP * (j + 1), CAP * m:CAP * (m + 1)] = hot
+
+    def stage_g(item, hot_ref, slot_ref, w_ref):
+        _, o, side = item_of(item)
+        g = jnp.dot(hot_ref[...], jmat[side, o], preferred_element_type=F32)
+        same = slot_ref[...] == slot_of(own[side, 1, pl.ds(o, 1), :])
+        w_ref[:, 0:CAP] = jnp.where(same, g[:, 0:CAP], 0.0).astype(BF16)
+        w_ref[:, CAP:] = jnp.where(same, g[:, CAP:], 0.0).astype(BF16)
+
+    def stage_u(item, w_ref, u_ref):
+        _, o, side = item_of(item)
+        u = lax.dot_general(w_ref[...], amat[side, o], (((1,), (1,)), ((), ())), preferred_element_type=F32)
         for j in range(GROUP):
-            same = slots[j] == mine
-            part = g[CAP * j:CAP * (j + 1)]
-            ws.append(jnp.concatenate(
-                [jnp.where(same, part[:, 0:CAP], 0.0).astype(BF16), jnp.where(same, part[:, CAP:], 0.0).astype(BF16)],
-                axis=1,
-            ))
-        u = lax.dot_general(
-            jnp.concatenate(ws, axis=0), amat[side, o], (((1,), (1,)), ((), ())), preferred_element_type=F32
-        )
+            high, low = split(u[CAP * j:CAP * (j + 1)])
+            u_ref[j, 0:CAP, :] = high
+            u_ref[j, CAP:, :] = low
+
+    def stage_t(item, u_ref):
+        p, o, _ = item_of(item)
         for j in range(GROUP):
             b = GROUP * p + j
-            uh, ul = split(u[CAP * j:CAP * (j + 1)])
             hot = one_hot_rows(oth[b, 0, pl.ds(o, 1), :], BLK, oth[b, 2, pl.ds(o, 1), :].astype(F32))
-            tacc[b] += jnp.dot(
-                jnp.concatenate([hot, hot], axis=1), jnp.concatenate([uh, ul], axis=0), preferred_element_type=F32
-            )
-        at_step(it, slots_t)
+            tacc[b] += jnp.dot(jnp.concatenate([hot, hot], axis=1), u_ref[j], preferred_element_type=F32)
+
+    stage_hot(jnp.int32(0), hot_0, slot_0)
+
+    def t_step(n, carry):
+        hots, slot_refs, ws, us = (hot_0, hot_1), (slot_0, slot_1), (w_0, w_1), (u_0, u_1)
+        for d in range(2):
+            it, e = 2 * n + d, 1 - d
+            stage_t(it - 2, us[d])
+            stage_u(it - 1, ws[e], us[e])
+            stage_g(it, hots[d], slot_refs[d], ws[d])
+            stage_hot(it + 1, hots[e], slot_refs[e])
+        at_step(n, slots_t)
         return carry
 
     lax.fori_loop(0, N_T, t_step, 0)
@@ -505,7 +528,15 @@
             pltpu.VMEM((blocks, 3, LISTS, CAP), I32),
             pltpu.VMEM((2, LISTS, PPAD, 2 * CAP), BF16),
             pltpu.VMEM((2, LISTS, BLK, 2 * CAP), BF16),
-            pltpu.VMEM((blocks, LISTS, CAP, CAP), I32),
+            pltpu.VMEM((blocks, CAP, CAP), I32),
+            pltpu.VMEM((GROUP * CAP, PPAD), BF16),
+            pltpu.VMEM((GROUP * CAP, PPAD), BF16),
+            pltpu.VMEM((GROUP * CAP, CAP), I32),
+            pltpu.VMEM((GROUP * CAP, CAP), I32),
+            pltpu.VMEM((GROUP * CAP, 2 * CAP), BF16),
+            pltpu.VMEM((GROUP * CAP, 2 * CAP), BF16),
+            pltpu.VMEM((GROUP, 2 * CAP, BLK), BF16),
+            pltpu.VMEM((GROUP, 2 * CAP, BLK), BF16),
             pltpu.VMEM((blocks, BLK, BLK), F32),
             pltpu.VMEM((BLK, BLK), F32),
             pltpu.SemaphoreType.DMA((10,)),

time: 99.7 us -> 76.1 us (0.76)
  Pallas kernels: 95.9 us -> 72.2 us
    pallas_call x1, Pallas kernels: 95.9 us -> 72.2 us  [shards(): pl.pallas_call(functools.partial(kernel, plan), out_shape=(out, out), in_...]
where the time goes in v3:
time: 76.1 us; the launch traced here: 75.9 us
  Pallas kernels  72.2 us (95%)
  local copies, waits for them, and re-layouts  2.42 us (3%)
  between operations  1.3 us (2%)
    pallas_call x1, Pallas kernels, shards(): pl.pallas_call(functools.partial(kernel, plan), out_shape=(out, out), in_...  72.2 us
    unnamed x4, local copies, waits for them, and re-layouts  2.42 us

profile of v3, /device:TPU:1, one launch (start us, length us, event | category | flops | bytes accessed | tf_op | source)
XLA Modules:
  0.0 75.9 jit_solution(7372309769568441174)
XLA Ops:
  1.3 72.2 %shard_map.113 = (f32[256,256]{1,0:T(8,128)}, f32[256,256]{1,0:T(8,128)}) custom-call(f32[1]{0:T(128)S(6)} %copy.14.shift_ref, f32[256,256]{1,0:T(8,128)} %c_ref.1, f32[256,256]{1,0:T(8,128)} %diag_ref.1, f32[484,484]{1,0:T(8,128)} %int_ref.1, s32[16,128]{1,0:T(8,128)} %src_r.1, s32[16,128]{1,0:T(8,128)} %tgt_r.1, s32[16,128]{1,0:T(8,128)} %ph_r.1, ...), custom_call_target="tpu_custom_call" | custom-call | tf_op jit(solution)/shard_map/pallas_call | solution.py:515
  73.5 0.0 copy-start
  73.5 1.7 %copy.15 = f32[256,256]{1,0:T(8,128)} copy(f32[256,256]{1,0:T(8,128)} %get-tuple-element.4) | data formatting | bytes 524288
  75.2 0.0 copy-done
  75.2 0.7 copy.16
Async XLA Ops:
  73.5 1.7 %copy-start = (f32[256,256]{1,0:T(8,128)S(1)}, f32[256,256]{1,0:T(8,128)}, u32[]{:S(2)}) copy-start(f32[256,256]{1,0:T(8,128)} %get-tuple-element.5) | copy-start | bytes 786436

commit v4 on v3

--- a/solution.py
+++ b/solution.py
@@ -101,11 +101,11 @@
     return copies
 
 
-RATE = {"x": 46.8, "y": 46.8, "z": 46.8, "s": 350.0}
-HOP = 1.8
-
-
-def simulate(copies, own_time):
+RATE = {"x": 44.0, "y": 44.0, "z": 44.0, "s": 300.0}
+HOP = 2.2
+
+
+def simulate(copies, own_time, handled):
     free, arrivals, pending = {}, {}, list(copies)
     while pending:
         best = None
@@ -119,7 +119,7 @@
         start = max(t, free.get(copy.way, 0.0))
         lasting = copy.rows[1] * BLK * 4 / RATE[copy.way[0]] / 1e3
         free[copy.way] = start + lasting
-        arrivals[copy.number] = start + lasting + HOP
+        arrivals[copy.number] = handled(start + lasting + HOP)
         pending.remove(copy)
     return arrivals
 
@@ -128,9 +128,15 @@
 PHASES = 3
 N_J, J_US = 8, 0.8
 ITEMS = 16 * PHASES
-N_T, T_US = ITEMS // 2 + 1, 0.9
+N_T, T_US = ITEMS // 2 + 1, 1.16
 LIST_US = 5.0
 T0_US = N_J * J_US + 1.5
+C_US = 0.0
+SLOTS = [(n + 1) * J_US for n in range(N_J)] + [T0_US + (n + 1) * T_US for n in range(N_T)]
+
+
+def handled(when):
+    return next((slot for slot in SLOTS if slot >= when), when)
 
 
 def make_plan():
@@ -138,10 +144,10 @@
     copies = plane_copies() + ring + block_copies(last)
     for n, copy in enumerate(copies):
         copy.number = n
-    own_time = {"C": 0.0}
+    own_time = {"C": C_US}
     for p in range(PHASES):
         own_time["T%d" % p] = T0_US + (8 * p + 9) * T_US
-    arrivals = simulate(copies, own_time)
+    arrivals = simulate(copies, own_time, handled)
     events = sorted(copies, key=lambda c: (arrivals[c.number], c.number))
     ready = {}
     for copy in copies:
@@ -190,18 +196,25 @@
     def flip(v, by):
         return 1 - v if by else v
 
+    xs = [lax.rem(x + d, NX) * NY for d in range(NX)]
+    ys = [lax.rem(y + d, NY) for d in range(NY)]
+    zs = [lax.rem(z + d, NZ) * 2 for d in range(NZ)]
+    ks = [k, 1 - k]
+    rows_at = {(i, j): xs[i] + ys[j] for i in range(NX) for j in range(NY)}
+    cols_at = {(i, j): zs[i] + ks[j] for i in range(NZ) for j in range(2)}
+    x_base = [2 * GROUP * flip(xpar, i) for i in range(2)]
+    z_base = {(i, j): 2 * GROUP * flip(zpar, i) + GROUP * ks[j] for i in range(2) for j in range(2)}
+
     def row_at(dx, dy):
-        return lax.rem(x + (dx + NX) % NX, NX) * NY + lax.rem(y + (dy + NY) % NY, NY)
+        return rows_at[(dx % NX, dy % NY)]
 
     def col_at(dz, by):
-        return lax.rem(z + (dz + NZ) % NZ, NZ) * 2 + flip(k, by)
+        return cols_at[(dz % NZ, by)]
 
     def place(buf, q, rel):
         if q == 0:
             return row_at(*rel) if buf == "x" else col_at(*rel)
-        if buf == "x":
-            return 2 * GROUP * flip(xpar, rel[0]) + rel[1]
-        return 2 * GROUP * flip(zpar, rel[0]) + GROUP * flip(k, rel[1]) + rel[2]
+        return x_base[rel[0]] + rel[1] if buf == "x" else z_base[rel[:2]] + rel[2]
 
     def device(way):
         if way == "s":
@@ -250,15 +263,34 @@
         return out
 
     def at_step(it, slots):
-        for n, evs in slots.items():
-            if evs:
-                @pl.when(it == n)
-                def _(evs=evs):
-                    for copy in evs:
-                        if callable(copy):
-                            copy()
-                        else:
-                            take(copy)
+        def act(evs):
+            for event in evs:
+                if callable(event):
+                    event()
+                else:
+                    take(event)
+
+        def walk(low, high):
+            filled = [n for n in range(low, high) if slots[n]]
+            if not filled:
+                return
+            if high - low == 1:
+                act(slots[low])
+                return
+            if len(filled) == 1:
+                pl.when(it == filled[0])(lambda: act(slots[filled[0]]))
+                return
+            mid = filled[len(filled) // 2]
+
+            def lower():
+                walk(low, mid)
+
+            def upper():
+                walk(mid, high)
+
+            lax.cond(it < mid, lower, upper)
+
+        walk(0, len(slots))
 
     lists = (src_r, tgt_r, ph_r, src_c, tgt_c, ph_c)
     loads = [pltpu.make_async_copy(lists[n], own.at[n // 3, n % 3], load_sem.at[n]) for n in range(6)]

time: 76.1 us -> 70.5 us (0.926)
  Pallas kernels: 72.2 us -> 66.6 us
    pallas_call x1, Pallas kernels: 72.2 us -> 66.6 us  [shards(): pl.pallas_call(functools.partial(kernel, plan), out_shape=(out, out), in_...]
where the time goes in v4:
time: 70.5 us; the launch traced here: 70.4 us
  Pallas kernels  66.6 us (94%)
  local copies, waits for them, and re-layouts  2.42 us (3%)
  between operations  1.3 us (2%)
    pallas_call x1, Pallas kernels, shards(): pl.pallas_call(functools.partial(kernel, plan), out_shape=(out, out), in_...  66.6 us
    unnamed x4, local copies, waits for them, and re-layouts  2.42 us

profile of v4, /device:TPU:1, one launch (start us, length us, event | category | flops | bytes accessed | tf_op | source)
XLA Modules:
  0.0 70.4 jit_solution(3591551700581443039)
XLA Ops:
  1.3 66.6 %shard_map.113 = (f32[256,256]{1,0:T(8,128)}, f32[256,256]{1,0:T(8,128)}) custom-call(f32[1]{0:T(128)S(6)} %copy.14.shift_ref, f32[256,256]{1,0:T(8,128)} %c_ref.1, f32[256,256]{1,0:T(8,128)} %diag_ref.1, f32[484,484]{1,0:T(8,128)} %int_ref.1, s32[16,128]{1,0:T(8,128)} %src_r.1, s32[16,128]{1,0:T(8,128)} %tgt_r.1, s32[16,128]{1,0:T(8,128)} %ph_r.1, ...), custom_call_target="tpu_custom_call" | custom-call | tf_op jit(solution)/shard_map/pallas_call | solution.py:547
  67.9 0.0 copy-start
  67.9 1.7 %copy.15 = f32[256,256]{1,0:T(8,128)} copy(f32[256,256]{1,0:T(8,128)} %get-tuple-element.4) | data formatting | bytes 524288
  69.6 0.0 copy-done
  69.7 0.7 copy.16
Async XLA Ops:
  67.9 1.7 %copy-start = (f32[256,256]{1,0:T(8,128)S(1)}, f32[256,256]{1,0:T(8,128)}, u32[]{:S(2)}) copy-start(f32[256,256]{1,0:T(8,128)} %get-tuple-element.5) | copy-start | bytes 786436

commit v5 on v4

--- a/solution.py
+++ b/solution.py
@@ -101,8 +101,8 @@
     return copies
 
 
-RATE = {"x": 44.0, "y": 44.0, "z": 44.0, "s": 300.0}
-HOP = 2.2
+RATE = {"x": 38.0, "y": 38.0, "z": 38.0, "s": 300.0}
+HOP = 3.5
 
 
 def simulate(copies, own_time, handled):

time: 70.5 us -> 67.3 us (0.955)
  Pallas kernels: 66.6 us -> 63.5 us
    pallas_call x1, Pallas kernels: 66.6 us -> 63.5 us  [shards(): pl.pallas_call(functools.partial(kernel, plan), out_shape=(out, out), in_...]
where the time goes in v5:
time: 67.3 us; the launch traced here: 67.2 us
  Pallas kernels  63.5 us (94%)
  local copies, waits for them, and re-layouts  2.42 us (4%)
  between operations  1.3 us (2%)
    pallas_call x1, Pallas kernels, shards(): pl.pallas_call(functools.partial(kernel, plan), out_shape=(out, out), in_...  63.5 us
    unnamed x4, local copies, waits for them, and re-layouts  2.42 us

profile of v5, /device:TPU:1, one launch (start us, length us, event | category | flops | bytes accessed | tf_op | source)
XLA Modules:
  0.0 67.2 jit_solution(17307894126064811247)
XLA Ops:
  1.3 63.5 %shard_map.113 = (f32[256,256]{1,0:T(8,128)}, f32[256,256]{1,0:T(8,128)}) custom-call(f32[1]{0:T(128)S(6)} %copy.14.shift_ref, f32[256,256]{1,0:T(8,128)} %c_ref.1, f32[256,256]{1,0:T(8,128)} %diag_ref.1, f32[484,484]{1,0:T(8,128)} %int_ref.1, s32[16,128]{1,0:T(8,128)} %src_r.1, s32[16,128]{1,0:T(8,128)} %tgt_r.1, s32[16,128]{1,0:T(8,128)} %ph_r.1, ...), custom_call_target="tpu_custom_call" | custom-call | tf_op jit(solution)/shard_map/pallas_call | solution.py:547
  64.8 0.0 copy-start
  64.8 1.7 %copy.15 = f32[256,256]{1,0:T(8,128)} copy(f32[256,256]{1,0:T(8,128)} %get-tuple-element.4) | data formatting | bytes 524288
  66.5 0.0 copy-done
  66.5 0.7 %copy.16 = f32[256,256]{1,0:T(8,128)} copy(f32[256,256]{1,0:T(8,128)S(1)} %copy-done) | data formatting | bytes 524288
Async XLA Ops:
  64.8 1.7 %copy-start = (f32[256,256]{1,0:T(8,128)S(1)}, f32[256,256]{1,0:T(8,128)}, u32[]{:S(2)}) copy-start(f32[256,256]{1,0:T(8,128)} %get-tuple-element.5) | copy-start | bytes 786436
